TPU v7x, 32 devices: a whole 2x2x4 slice. The times are simulated.
32 devices in a mesh: segment: 2 (over core), clip: 4 (over z), tile: 4 (over y, x).
Axes of the slice: x: 2, y: 2, z: 4, core: 2. Of those that a mesh axis runs over, the one named last changes fastest.
Arguments:
- video: bfloat16 [4, 4, 3, 12, 4, 256], P('clip', 'tile'), may hold values from -6 to 6
- cotangent: bfloat16 [4, 4, 3, 12, 4, 256], P('clip', 'tile'), may hold values from -6 to 6
- weights: bfloat16 [2, 27, 256, 256], P('segment'), may hold values from -0.078125 to 0.078125
- neighbours: int32 [4, 4, 2], P('clip', 'tile'), may hold values from 0 to 4, as said below
- rows_used: int32 [4, 4], P('clip', 'tile'), may hold values from 3 to 12, as said below
- cols_used: int32 [4], P('clip'), may hold values from 2 to 4, as said below
Outputs:
- section_out: bfloat16 [2, 4, 4, 3, 12, 4, 256], P('segment', 'clip', 'tile')
- grads: float32 [2, 3, 589824], P('segment', None, ('clip', 'tile'))
Inputs may be any that keep to these rules, and one draw needn't show every extreme that they name: `neighbours`: in each clip the strips of its frames lie on the 4 tiles in an order of their own: entry 0 names the tile of the strip above, entry 1 the tile of the strip below, 4 where there is none; exactly one strip of each clip has none above and one has none below, and the entries chain all 4 strips of a clip top to bottom. `rows_used`: in every clip some strip has 12 rows. `cols_used`: some clip has 4 columns.
All inputs are finite; a program needn't handle non-finite values.
Results may differ from a plain program's by a relative error of at most 0.0054.
Values may be sent and summed in bfloat16 or wider, within the bound.
A program may use at most 576 MiB of HBM per device.

v0:
```python
import jax
import jax.numpy as jnp
from jax import lax
from jax.sharding import PartitionSpec as P


def shifted(block, axis, distance):
    devices = range(lax.axis_size(axis))
    route = [(i - distance, i) for i in devices if i - distance in devices]
    return lax.ppermute(block, axis, route)


def silu_grad(values):
    sigmoid = jax.nn.sigmoid(values)
    return sigmoid * (1.0 + values * (1.0 - sigmoid))


def pad_block(strip_field, upper, bottom, row_count):
    frame_count, height, columns, channels = strip_field.shape
    blank = jnp.zeros((frame_count, 1, columns, channels), strip_field.dtype)
    padded = jnp.concatenate([upper[:, None], strip_field, blank], axis=1)
    padded = lax.dynamic_update_slice_in_dim(padded, bottom[:, None], row_count + 1, axis=1)
    return jnp.pad(padded, ((0, 0), (0, 0), (1, 1), (0, 0)))


def patches(stacked, frame_count, height, columns):
    pieces = []
    for depth_off in range(3):
        for row_off in range(3):
            for col_off in range(3):
                pieces.append(
                    stacked[
                        depth_off : depth_off + frame_count,
                        row_off : row_off + height,
                        col_off : col_off + columns,
                    ]
                )
    return jnp.concatenate(pieces, axis=-1).reshape(frame_count * height * columns, -1)


def own_entries(padded, weighting, axes):
    frame_count, tall, columns, channels = padded.shape
    height = tall - 2
    payload = jnp.concatenate([padded.reshape(-1, channels), weighting], axis=0)
    gathered = lax.all_gather(payload, axes, axis=0)
    cut = frame_count * tall * columns
    strips = gathered[:, :cut].reshape(-1, frame_count, tall, columns, channels)
    strips = jnp.pad(strips, ((0, 0), (2, 0), (0, 0), (1, 1), (0, 0)))
    upstream = gathered[:, cut:].reshape(-1, channels)
    row_total = 9 * channels // lax.axis_size(axes)
    start = lax.axis_index(axes) * row_total
    low = jnp.minimum(start // channels, 8)
    lower = []
    for step in range(-(-row_total // channels) + 1):
        tap = jnp.minimum(low + step, 8)
        lower.append(
            lax.dynamic_slice(
                strips,
                (0, 0, tap // 3, tap % 3, 0),
                (strips.shape[0], frame_count + 2, height, columns, channels),
            )
        )
    window = jnp.concatenate(lower, axis=-1)
    window = lax.dynamic_slice_in_dim(window, start - low * channels, row_total, 4)
    contract = (((0,), (0,)), ((), ()))
    return jnp.stack(
        [
            lax.dot_general(
                window[:, tap : tap + frame_count].reshape(-1, row_total),
                upstream,
                contract,
                preferred_element_type=jnp.float32,
            ).reshape(-1)
            for tap in range(3)
        ]
    )


def local(video, cotangent, weights, neighbours, rows_used, cols_used):
    window = video[0, 0]
    frame_count, height, columns, channels = window.shape
    tile_count = lax.axis_size("tile")
    section = lax.axis_index("segment")
    row_count = rows_used[0, 0]
    col_count = cols_used[0]
    upper_tile = neighbours[0, 0, 0]
    lower_tile = neighbours[0, 0, 1]
    row_ids = jnp.arange(height, dtype=jnp.int32)
    col_ids = jnp.arange(columns, dtype=jnp.int32)
    inside = (row_ids[:, None] < row_count) & (col_ids[None, :] < col_count)
    inside_mask = inside[None, :, :, None]
    kernel = weights[0]
    forward_mat = kernel.reshape(27 * channels, channels)
    backward_mat = kernel[::-1].transpose(0, 2, 1).reshape(27 * channels, channels)
    front_zero = jnp.zeros((2, height + 2, columns + 2, channels), jnp.bfloat16)

    def halo_block(field):
        leading = field[:, 0]
        trailing = lax.dynamic_index_in_dim(field, row_count - 1, axis=1, keepdims=False)
        both_rows = jnp.stack([leading, trailing], axis=1)
        gathered = lax.all_gather(both_rows[None], "tile", axis=0, tiled=True)
        upper = gathered[jnp.minimum(upper_tile, tile_count - 1), :, 1]
        bottom = gathered[jnp.minimum(lower_tile, tile_count - 1), :, 0]
        upper = jnp.where(upper_tile < tile_count, upper, jnp.zeros_like(upper))
        bottom = jnp.where(lower_tile < tile_count, bottom, jnp.zeros_like(bottom))
        return pad_block(field, upper, bottom, row_count)

    def advance(entry, history):
        count = entry.shape[0]
        activated = jax.nn.silu(entry.astype(jnp.float32)).astype(jnp.bfloat16)
        padded = halo_block(activated)
        stacked = jnp.concatenate([history, padded], axis=0)
        mixed = jnp.dot(
            patches(stacked, count, height, columns),
            forward_mat,
            preferred_element_type=jnp.float32,
        ).reshape(entry.shape)
        result = jnp.where(inside_mask, entry.astype(jnp.float32) + mixed, 0.0).astype(jnp.bfloat16)
        return (result, stacked[-2:], padded)

    source = jnp.where(inside_mask, window, jnp.zeros_like(window))
    is_encoder = section == 0
    first_out, first_hist, first_pad = advance(source, front_zero)
    latent = shifted(first_out, "segment", 1)
    second_out, second_hist, second_pad = advance(latent, front_zero)
    own_out = jnp.where(is_encoder, first_out, second_out)
    own_input = jnp.where(is_encoder, source, latent)
    own_pad = jnp.where(is_encoder, first_pad, second_pad)
    target = jnp.where(inside_mask, cotangent[0, 0], jnp.zeros_like(cotangent[0, 0]))
    back_stack = jnp.concatenate([halo_block(target), front_zero], axis=0)
    spread = jnp.dot(
        patches(back_stack, frame_count, height, columns),
        backward_mat,
        preferred_element_type=jnp.float32,
    ).reshape(target.shape)
    own_grad = jnp.where(
        inside_mask,
        target.astype(jnp.float32) + silu_grad(own_input.astype(jnp.float32)) * spread,
        0.0,
    ).astype(jnp.bfloat16)
    returned = shifted(own_grad, "segment", -1)
    weighting = jnp.where(is_encoder, returned, target).reshape(-1, channels)
    summed = own_entries(own_pad[:, :, 1:-1], weighting, ("clip", "tile"))
    return (own_out[None, None, None], summed[None])


def solution(mesh):
    in_specs = (
        P("clip", "tile", None, None, None, None),
        P("clip", "tile", None, None, None, None),
        P("segment", None, None, None),
        P("clip", "tile", None),
        P("clip", "tile"),
        P("clip"),
    )
    out_specs = (
        P("segment", "clip", "tile", None, None, None, None),
        P("segment", None, ("clip", "tile")),
    )
    return jax.shard_map(local, mesh=mesh, in_specs=in_specs, out_specs=out_specs, check_vma=False)
```

profile of v0, /device:TPU:0, one launch (start us, length us, event | category | flops | bytes accessed | tf_op | source)
XLA Modules:
  0.0 162.4 jit_solution(4665979440617564632)
XLA Ops:
  7.2 0.0 all-gather.6.cloned.1.call-start
  7.2 1.3 fusion.28
  12.4 0.1 broadcast_and_fusion
  12.5 1.0 bitcast_select_fusion
  13.5 1.0 fusion.19
  14.6 9.7 %all-gather = bf16[12,2,4,256]{3,2,1,0:T(4,128)(2,1)S(1)} all-gather(bf16[3,2,4,256]{3,2,1,0:T(4,128)(2,1)S(1)} %copy.132), channel_id=2, replica_groups=mesh['segment'=2,'clip'=4,'tile'=4] {'tile'}, dimensions={0}, use_global_device_ids=true | all-gather | bytes 61440 | tf_op jit(solution)/shard_map/all_gather | solution.py:101
  24.4 8.2 %all-gather.2 = bf16[12,2,4,256]{3,2,1,0:T(4,128)(2,1)S(1)} all-gather(bf16[3,2,4,256]{3,2,1,0:T(4,128)(2,1)S(1)} %copy.140), channel_id=4, replica_groups=mesh['segment'=2,'clip'=4,'tile'=4] {'tile'}, dimensions={0}, use_global_device_ids=true | all-gather | bytes 61440 | tf_op jit(solution)/shard_map/all_gather | solution.py:101
  32.7 0.1 pad.40.clone
  32.8 0.1 maximum_maximum_fusion.2
  32.9 0.1 dynamic_update_slice.9
  33.7 1.4 copy-done
  35.0 0.9 fusion.3
  35.9 1.3 collective-permute-start
  37.2 0.1 dynamic_update_slice.11
  37.3 5.8 %copy.143 = bf16[1,27,256,256]{2,3,1,0:T(8,128)(2,1)} copy(bf16[1,27,256,256]{3,2,1,0:T(8,128)(2,1)} %param.8) | data formatting | bytes 7077888 | tf_op args[2]
  43.7 4.2 %rev.3 = bf16[27,256,256]{1,2,0:T(8,128)(2,1)} reverse(bf16[27,256,256]{1,2,0:T(8,128)(2,1)} %bitcast.88), dimensions={0} | reverse | bytes 7077888 | tf_op jit(solution)/shard_map/rev | solution.py:94
  48.0 3.0 %fusion.15 = (bf16[3,12,4,256]{3,1,2,0:T(8,128)(2,1)S(1)}, bf16[3,12,4,256]{3,1,2,0:T(8,128)(2,1)S(1)}) fusion(bf16[3,12,4,256]{3,1,2,0:T(8,128)(2,1)S(1)} %collective-permute-done, pred[12,4]{0,1:T(4,128)(4,1)S(1)} %broadcast_and_fusion, pred[]{:T(512)S(6)} %eq.6, bf16[1,1,3,12,4,256]{5,4,3,2,1,0:T(4,128)(2,1)S(1)} %copy-done.5, ...), kind=kOutput, calls=%fused_computation.85 | convolution fusion | flops 510418944 | bytes 5898289 | tf_op jit(solution)/shard_map/dot_general | solution.py:131
  51.0 7.3 %all-gather.1 = bf16[12,2,4,256]{3,2,1,0:T(4,128)(2,1)S(1)} all-gather(bf16[3,2,4,256]{3,2,1,0:T(4,128)(2,1)S(1)} %copy.135), channel_id=3, replica_groups=mesh['segment'=2,'clip'=4,'tile'=4] {'tile'}, dimensions={0}, use_global_device_ids=true | all-gather | bytes 61440 | tf_op jit(solution)/shard_map/all_gather | solution.py:101
  58.4 0.1 maximum_maximum_fusion.1
  58.5 1.3 collective-permute-start.1
  59.8 0.1 dynamic_update_slice.10
  59.9 1.7 %collective-permute-done.1 = bf16[3,12,4,256]{3,1,2,0:T(8,128)(2,1)S(1)} collective-permute-done((bf16[3,12,4,256]{3,1,2,0:T(8,128)(2,1)S(1)}, bf16[3,12,4,256]{3,1,2,0:T(8,128)(2,1)S(1)}, u32[]{:S(2)}, u32[]{:S(2)}) %collective-permute-start.1) | collective-permute-done | bytes 73760 | tf_op jit(solution)/shard_map/ppermute | solution.py:10
  61.7 0.1 broadcast_select_fusion
  61.8 0.7 pad_maximum_fusion.1
  62.5 0.0 all-gather.6.cloned.1.call-update
  63.3 1.4 copy-done.1
  64.7 0.9 fusion.6
  65.6 0.7 copy.145
  66.3 60.1 %all-gather.6.cloned.1.call-done = bf16[4992,256]{1,0:T(8,128)(2,1)} async-done(((bf16[312,256]{1,0:T(8,128)(2,1)}), bf16[4992,256]{1,0:T(8,128)(2,1)}) %all-gather.6.cloned.1.call-update) | async-done | bytes 2555920 | tf_op jit(solution)/shard_map/all_gather | solution.py:45
  126.4 2.5 %slice.389 = bf16[16,168,256]{2,1,0:T(8,128)(2,1)} slice(bf16[16,312,256]{2,1,0:T(8,128)(2,1)} %bitcast.90), slice={[0:16], [0:168], [0:256]} | slice | bytes 2752512 | tf_op jit(solution)/shard_map/slice | solution.py:47
  128.9 1.3 slice.391
  130.2 2.9 %reshape.170 = bf16[16,3,14,4,256]{4,3,2,1,0:T(4,128)(2,1)S(1)} reshape(bf16[16,168,256]{2,1,0:T(8,128)(2,1)} %slice.389) | data formatting | bytes 2752512 | tf_op jit(solution)/shard_map/reshape | solution.py:47
  133.1 3.5 %pad_dynamic-slice_fusion = (bf16[16,5,12,4,256]{4,3,2,1,0:T(4,128)(2,1)S(1)}, bf16[16,5,12,4,256]{4,3,2,1,0:T(4,128)(2,1)S(1)}) fusion(s32[]{:T(128)S(6)} %select_n.223, s32[]{:T(128)S(6)} %select_n.225, bf16[16,3,14,4,256]{4,3,2,1,0:T(4,128)(2,1)S(1)} %reshape.170, s32[]{:T(128)S(6)} %select_n.219, s32[]{:T(128)S(6)} %select_n.221), kind=kLoop, calls=%fused_computation | loop fusion | bytes 5308432 | tf_op jit(solution)/shard_map/dynamic_slice | solution.py:57
  136.6 3.8 %fusion = bf16[16,5,12,4,144]{4,3,2,1,0:T(4,128)(2,1)S(1)} fusion(s32[]{:T(128)S(6)} %select_n.226, bf16[16,5,12,4,256]{4,3,2,1,0:T(4,128)(2,1)S(1)} %get-tuple-element.22, bf16[16,5,12,4,256]{4,3,2,1,0:T(4,128)(2,1)S(1)} %get-tuple-element.21), kind=kLoop, calls=%fused_computation.4 | loop fusion | flops 2211840 | bytes 5038084 | tf_op jit(solution)/shard_map/concatenate | solution.py:63
  140.4 2.1 %fusion.24 = (bf16[16,3,12,4,144]{4,3,2,1,0:T(4,128)(2,1)}, bf16[16,3,12,4,144]{4,3,2,1,0:T(4,128)(2,1)S(1)}, bf16[16,3,12,4,144]{4,3,2,1,0:T(4,128)(2,1)S(1)}) fusion(bf16[16,5,12,4,144]{4,3,2,1,0:T(4,128)(2,1)S(1)} %fusion), kind=kLoop, calls=%fused_computation.198 | loop fusion | bytes 3981312 | tf_op jit(solution)/shard_map/slice | solution.py:69
  142.5 3.2 %reshape.171 = bf16[2304,144]{1,0:T(8,128)(2,1)} reshape(bf16[16,3,12,4,144]{4,3,2,1,0:T(4,128)(2,1)} %get-tuple-element.18) | data formatting | bytes 1327104 | tf_op jit(solution)/shard_map/reshape | solution.py:69
  145.7 1.7 %convolution_bitcast_fusion.2 = f32[1,1,144,256]{3,2,1,0:T(8,128)S(1)} fusion(bf16[2304,144]{1,0:T(8,128)(2,1)} %reshape.171, bf16[2304,256]{1,0:T(8,128)(2,1)S(1)} %bitcast.83), kind=kOutput, calls=%fused_computation.11 | convolution fusion | flops 169869312 | bytes 1990656 | tf_op jit(solution)/shard_map/dot_general | solution.py:68
  147.4 0.8 copy.148
  148.2 1.6 reshape.173
  149.8 1.7 %convolution_bitcast_fusion.1 = f32[1,1,144,256]{3,2,1,0:T(8,128)S(1)} fusion(bf16[2304,144]{1,0:T(8,128)(2,1)} %reshape.173, bf16[2304,256]{1,0:T(8,128)(2,1)S(1)} %bitcast.84), kind=kOutput, calls=%fused_computation.10 | convolution fusion | flops 169869312 | bytes 1990656 | tf_op jit(solution)/shard_map/dot_general | solution.py:68
  151.6 0.8 copy.149
  152.4 0.7 reshape.174
  153.1 0.5 convolution_bitcast_fusion
  153.6 0.2 copy.150
  153.8 0.3 copy-done.2
  154.0 0.1 copy-done.3
  154.1 0.4 pad_maximum_fusion
  154.5 1.1 broadcast_in_dim.60
  (117 shorter events, 1.9 us)
Async XLA Ops:
  7.2 119.2 %all-gather.6.cloned.1.call-start = ((), (), s32[]{:S(2)}) async-start(), calls=%async_computation | async-start | bytes 2715648 | tf_op jit(solution)/shard_map/all_gather | solution.py:45
  33.0 2.0 %copy-start = (bf16[1,27,256,256]{3,2,1,0:T(8,128)(2,1)S(1)}, bf16[1,27,256,256]{3,2,1,0:T(8,128)(2,1)}, u32[]{:S(2)}) copy-start(bf16[1,27,256,256]{3,2,1,0:T(8,128)(2,1)} %param.8) | copy-start | bytes 10616836
  33.0 2.0 %copy-start.5 = (bf16[1,1,3,12,4,256]{5,4,3,2,1,0:T(4,128)(2,1)S(1)}, bf16[1,1,3,12,4,256]{5,4,3,2,1,0:T(4,128)(2,1)}, u32[]{:S(2)}) copy-start(bf16[1,1,3,12,4,256]{5,4,3,2,1,0:T(4,128)(2,1)} %param.6) | copy-start | bytes 221188
  35.9 12.1 %collective-permute-start = (bf16[3,12,4,256]{3,1,2,0:T(8,128)(2,1)S(1)}, bf16[3,12,4,256]{3,1,2,0:T(8,128)(2,1)S(1)}, u32[]{:S(2)}, u32[]{:S(2)}) collective-permute-start(bf16[3,12,4,256]{3,1,2,0:T(8,128)(2,1)S(1)} %fusion.3), channel_id=1, source_target_pairs={{0,16},{1,17},{2,18},{3,19},{4,20},{5,21},{6,22},{7,23},{8,24},{9,... | collective-permute-start | bytes 221192 | tf_op jit(solution)/shard_map/ppermute | solution.py:10
  43.7 4.3 %copy-start.4 = (bf16[1,1,3,12,4,256]{5,4,3,2,1,0:T(4,128)(2,1)S(1)}, bf16[1,1,3,12,4,256]{5,4,3,2,1,0:T(4,128)(2,1)}, u32[]{:S(2)}) copy-start(bf16[1,1,3,12,4,256]{5,4,3,2,1,0:T(4,128)(2,1)} %param.7) | copy-start | bytes 221188
  58.5 3.2 %collective-permute-start.1 = (bf16[3,12,4,256]{3,1,2,0:T(8,128)(2,1)S(1)}, bf16[3,12,4,256]{3,1,2,0:T(8,128)(2,1)S(1)}, u32[]{:S(2)}, u32[]{:S(2)}) collective-permute-start(bf16[3,12,4,256]{3,1,2,0:T(8,128)(2,1)S(1)} %get-tuple-element.23), channel_id=1, source_target_pairs={{16,0},{17,1},{18,2},{19,3},{20,4},{21,5},{22,6},{23,7},{24,8},{25... | collective-permute-start | bytes 221192 | tf_op jit(solution)/shard_map/ppermute | solution.py:10
  62.7 2.0 %copy-start.1 = (bf16[1,27,256,256]{3,2,1,0:T(8,128)(2,1)S(1)}, bf16[1,27,256,256]{3,2,1,0:T(8,128)(2,1)}, u32[]{:S(2)}) copy-start(bf16[1,27,256,256]{3,2,1,0:T(8,128)(2,1)} %param.8) | copy-start | bytes 10616836
  153.1 0.9 copy-start.2
  153.1 1.0 copy-start.3
Sparse Core Ops, SparseCore 0:
  62.6 63.7 all-gather.5
where the time goes:
time: 163 us; the launch traced here: 162 us
  waiting for transfers between devices  61.8 us (38%)
  local copies, waits for them, and re-layouts  37.7 us (23%)
  blocking collectives  25.2 us (15%)
  between operations  19.1 us (12%)
  matrix products  8.63 us (5%)
  other arithmetic  7.39 us (5%)
  starting transfers between devices  2.62 us (2%)
    all_gather x1, waiting for transfers between devices, own_entries(): gathered = lax.all_gather(payload, axes, axis=0)  60.1 us
    all_gather x3, blocking collectives, halo_block(): gathered = lax.all_gather(both_rows[None], 'tile', axis=0, tiled=True)  25.2 us
    unnamed x95, local copies, waits for them, and re-layouts  12.6 us
    reshape x3, local copies, waits for them, and re-layouts, own_entries(): window[:, tap:tap + frame_count].reshape(-1, row_total)  5.48 us
    rev x1, local copies, waits for them, and re-layouts, local(): kernel[::-1].transpose(0, 2, 1).reshape(27 * channels, channels)  4.22 us
    dot_general x3, matrix products, own_entries(): lax.dot_general(window[:, tap:tap + frame_count].reshape(-1, row_total),...  3.94 us
    concatenate x1, other arithmetic, own_entries(): window = jnp.concatenate(lower, axis=-1)  3.82 us
    dynamic_slice x1, local copies, waits for them, and re-layouts, own_entries(): lax.dynamic_slice(strips, (0, 0, tap // 3, tap % 3, 0), (strips.shape[0],...  3.48 us
  transfers between devices with their start and end apart: 3, of which 2 were waited for; matrix products, arithmetic and copies ran while one was open for 8% of the time, Pallas kernels for 0%

commit v1 on v0

--- a/solution.py
+++ b/solution.py
@@ -2,6 +2,18 @@
 import jax.numpy as jnp
 from jax import lax
 from jax.sharding import PartitionSpec as P
+
+
+def gather_by_bits(x, axis, dim):
+    ways, here = (lax.axis_size(axis), lax.axis_index(axis))
+    grown, reach = (x, 1)
+    while reach < ways:
+        theirs = lax.ppermute(grown, axis, [(d, d ^ reach) for d in range(ways)])
+        mine_first = jnp.concatenate([grown, theirs], axis=dim)
+        theirs_first = jnp.concatenate([theirs, grown], axis=dim)
+        grown = jnp.where(here & reach == 0, mine_first, theirs_first)
+        reach = 2 * reach
+    return grown
 
 
 def shifted(block, axis, distance):
@@ -98,7 +110,7 @@
         leading = field[:, 0]
         trailing = lax.dynamic_index_in_dim(field, row_count - 1, axis=1, keepdims=False)
         both_rows = jnp.stack([leading, trailing], axis=1)
-        gathered = lax.all_gather(both_rows[None], "tile", axis=0, tiled=True)
+        gathered = gather_by_bits(both_rows[None], "tile", 0)
         upper = gathered[jnp.minimum(upper_tile, tile_count - 1), :, 1]
         bottom = gathered[jnp.minimum(lower_tile, tile_count - 1), :, 0]
         upper = jnp.where(upper_tile < tile_count, upper, jnp.zeros_like(upper))

time: 163 us -> 152 us (0.933)
  blocking collectives: 25.2 us -> 0 us
  waiting for transfers between devices: 61.8 us -> 69.8 us
  starting transfers between devices: 2.62 us -> 9.62 us
  other arithmetic: 7.39 us -> 11.1 us
  local copies, waits for them, and re-layouts: 37.7 us -> 35.3 us
  matrix products: 8.63 us -> 6.67 us
    all_gather x3 -> x0, blocking collectives: 25.2 us -> none  [halo_block(): gathered = lax.all_gather(both_rows[None], 'tile', axis=0, tiled=True)]
    ppermute x0 -> x6, waiting for transfers between devices: none -> 8.41 us  [gather_by_bits(): theirs = lax.ppermute(grown, axis, [(d, d ^ reach) for d in range(ways)])]
    ppermute x0 -> x6, starting transfers between devices: none -> 6.87 us  [gather_by_bits(): theirs = lax.ppermute(grown, axis, [(d, d ^ reach) for d in range(ways)])]
    rev x1, local copies, waits for them, and re-layouts: 4.22 us -> 1.98 us  [local(): kernel[::-1].transpose(0, 2, 1).reshape(27 * channels, channels)]
    select_n x0 -> x6, other arithmetic: none -> 2.06 us  [gather_by_bits(): grown = jnp.where(here & reach == 0, mine_first, theirs_first)]
    dot_general x1, matrix products: 2.96 us -> 0.97 us  [local(): jnp.dot(patches(back_stack, frame_count, height, columns), backward_mat,...]
    unnamed x95 -> x101, local copies, waits for them, and re-layouts: 12.6 us -> 12.6 us
  transfers between devices with their start and end apart: 3 -> 9, of which waited for: 2 -> 6; matrix products, arithmetic and copies ran while one was open for 8% -> 9% of each run, Pallas kernels for 0% -> 0%
where the time goes in v1:
time: 152 us; the launch traced here: 151 us
  waiting for transfers between devices  69.8 us (46%)
  local copies, waits for them, and re-layouts  35.3 us (23%)
  between operations  18.9 us (12%)
  other arithmetic  11.1 us (7%)
  starting transfers between devices  9.62 us (6%)
  matrix products  6.67 us (4%)
    all_gather x1, waiting for transfers between devices, own_entries(): gathered = lax.all_gather(payload, axes, axis=0)  60.5 us
    unnamed x101, local copies, waits for them, and re-layouts  12.6 us
    ppermute x6, waiting for transfers between devices, gather_by_bits(): theirs = lax.ppermute(grown, axis, [(d, d ^ reach) for d in range(ways)])  8.41 us
    ppermute x6, starting transfers between devices, gather_by_bits(): theirs = lax.ppermute(grown, axis, [(d, d ^ reach) for d in range(ways)])  6.87 us
    reshape x3, local copies, waits for them, and re-layouts, own_entries(): window[:, tap:tap + frame_count].reshape(-1, row_total)  5.46 us
    dot_general x3, matrix products, own_entries(): lax.dot_general(window[:, tap:tap + frame_count].reshape(-1, row_total),...  3.94 us
    concatenate x1, other arithmetic, own_entries(): window = jnp.concatenate(lower, axis=-1)  3.82 us
    dynamic_slice x1, local copies, waits for them, and re-layouts, own_entries(): lax.dynamic_slice(strips, (0, 0, tap // 3, tap % 3, 0), (strips.shape[0],...  3.48 us
  transfers between devices with their start and end apart: 9, of which 6 were waited for; matrix products, arithmetic and copies ran while one was open for 9% of the time, Pallas kernels for 0%

profile of v1, /device:TPU:0, one launch (start us, length us, event | category | flops | bytes accessed | tf_op | source)
XLA Modules:
  0.0 151.4 jit_solution(3532956533293618021)
XLA Ops:
  8.6 1.0 bitcast_select_fusion
  9.6 0.6 copy-done.5
  10.3 3.0 %collective-permute-start.5 = (bf16[1,3,2,4,256]{4,2,3,1,0:T(2,128)(2,1)S(1)}, bf16[1,3,2,4,256]{4,2,3,1,0:T(2,128)(2,1)}, u32[]{:S(2)}, u32[]{:S(2)}) collective-permute-start(bf16[1,3,2,4,256]{4,2,3,1,0:T(2,128)(2,1)S(1)} %maximum_bitcast_fusion.2), channel_id=1, source_target_pairs={{0,1},{1,0},{2,3},{3,2},{4,5},{5,4},{6,7},{7,6},{8,9},{9,8},{10,11... | collective-permute-start | bytes 36872 | tf_op jit(solution)/shard_map/ppermute | solution.py:11
  13.3 1.0 fusion.19
  14.3 0.6 copy-done.6
  15.0 0.6 maximum_bitcast_fusion
  15.6 1.3 fusion.34
  19.5 4.4 %copy.41 = bf16[1,27,256,256]{2,3,1,0:T(8,128)(2,1)S(1)} copy(bf16[1,27,256,256]{3,2,1,0:T(8,128)(2,1)} %param.8) | data formatting | bytes 7077888 | tf_op args[2]
  24.0 2.0 %rev.3 = bf16[27,256,256]{1,2,0:T(8,128)(2,1)} reverse(bf16[27,256,256]{1,2,0:T(8,128)(2,1)S(1)} %bitcast.91), dimensions={0} | reverse | bytes 7077888 | tf_op jit(solution)/shard_map/rev | solution.py:106
  26.0 0.8 broadcast_select_fusion.4
  26.8 2.1 %collective-permute-start.6 = (bf16[2,3,2,4,256]{4,2,3,1,0:T(2,128)(2,1)S(1)}, bf16[2,3,2,4,256]{4,2,3,1,0:T(2,128)(2,1)S(1)}, u32[]{:S(2)}, u32[]{:S(2)}) collective-permute-start(bf16[2,3,2,4,256]{4,2,3,1,0:T(2,128)(2,1)S(1)} %broadcast_select_fusion.4), channel_id=1, source_target_pairs={{0,2},{1,3},{2,0},{3,1},{4,6},{5,7},{6,4},{7,5},{8,10},{9,11},{10,... | collective-permute-start | bytes 73736 | tf_op jit(solution)/shard_map/ppermute | solution.py:11
  28.9 0.8 broadcast_select_fusion.6
  29.9 0.9 collective-permute-done.6
  30.8 0.1 broadcast_select_fusion
  30.9 2.8 %collective-permute-done.1 = bf16[2,3,2,4,256]{4,2,3,1,0:T(2,128)(2,1)S(1)} collective-permute-done((bf16[2,3,2,4,256]{4,2,3,1,0:T(2,128)(2,1)S(1)}, bf16[2,3,2,4,256]{4,2,3,1,0:T(2,128)(2,1)S(1)}, u32[]{:S(2)}, u32[]{:S(2)}) %collective-permute-start.1) | collective-permute-done | bytes 24608 | tf_op jit(solution)/shard_map/ppermute | solution.py:11
  33.9 1.1 maximum_maximum_fusion.2
  36.5 1.4 copy-done
  37.9 0.9 fusion.3
  38.7 1.4 collective-permute-start.2
  40.2 0.9 collective-permute-done.2
  41.1 1.0 fusion.15
  42.2 1.6 %collective-permute-start.3 = (bf16[1,3,2,4,256]{4,2,3,1,0:T(2,128)(2,1)S(1)}, bf16[1,3,2,4,256]{4,2,3,1,0:T(2,128)(2,1)S(1)}, u32[]{:S(2)}, u32[]{:S(2)}) collective-permute-start(bf16[1,3,2,4,256]{4,2,3,1,0:T(2,128)(2,1)S(1)} %maximum_bitcast_fusion.1), channel_id=1, source_target_pairs={{0,1},{1,0},{2,3},{3,2},{4,5},{5,4},{6,7},{7,6},{8,9},{9,8},{10,11... | collective-permute-start | bytes 36872 | tf_op jit(solution)/shard_map/ppermute | solution.py:11
  43.7 2.2 %collective-permute-done.3 = bf16[1,3,2,4,256]{4,2,3,1,0:T(2,128)(2,1)S(1)} collective-permute-done((bf16[1,3,2,4,256]{4,2,3,1,0:T(2,128)(2,1)S(1)}, bf16[1,3,2,4,256]{4,2,3,1,0:T(2,128)(2,1)S(1)}, u32[]{:S(2)}, u32[]{:S(2)}) %collective-permute-start.3) | collective-permute-done | bytes 12320 | tf_op jit(solution)/shard_map/ppermute | solution.py:11
  46.1 1.3 collective-permute-start.7
  47.4 2.5 %collective-permute-done.4 = bf16[2,3,2,4,256]{4,2,3,1,0:T(2,128)(2,1)S(1)} collective-permute-done((bf16[2,3,2,4,256]{4,2,3,1,0:T(2,128)(2,1)S(1)}, bf16[2,3,2,4,256]{4,2,3,1,0:T(2,128)(2,1)S(1)}, u32[]{:S(2)}, u32[]{:S(2)}) %collective-permute-start.4) | collective-permute-done | bytes 24608 | tf_op jit(solution)/shard_map/ppermute | solution.py:11
  50.5 0.7 pad_maximum_fusion.1
  52.0 1.4 copy-done.1
  53.4 0.9 fusion.6
  54.3 0.7 copy.43
  54.9 60.5 %all-gather.3.cloned.1.call-done = bf16[4992,256]{1,0:T(8,128)(2,1)} async-done(((bf16[312,256]{1,0:T(8,128)(2,1)}), bf16[4992,256]{1,0:T(8,128)(2,1)}) %all-gather.3.cloned.1.call-update) | async-done | bytes 2555920 | tf_op jit(solution)/shard_map/all_gather | solution.py:57
  115.4 2.5 %slice.389 = bf16[16,168,256]{2,1,0:T(8,128)(2,1)} slice(bf16[16,312,256]{2,1,0:T(8,128)(2,1)} %bitcast.93), slice={[0:16], [0:168], [0:256]} | slice | bytes 2752512 | tf_op jit(solution)/shard_map/slice | solution.py:59
  117.9 1.3 slice.391
  119.3 2.9 %reshape.170 = bf16[16,3,14,4,256]{4,3,2,1,0:T(4,128)(2,1)S(1)} reshape(bf16[16,168,256]{2,1,0:T(8,128)(2,1)} %slice.389) | data formatting | bytes 2752512 | tf_op jit(solution)/shard_map/reshape | solution.py:59
  122.2 3.5 %pad_dynamic-slice_fusion = (bf16[16,5,12,4,256]{4,3,2,1,0:T(4,128)(2,1)S(1)}, bf16[16,5,12,4,256]{4,3,2,1,0:T(4,128)(2,1)S(1)}) fusion(s32[]{:T(128)S(6)} %select_n.263, s32[]{:T(128)S(6)} %select_n.265, bf16[16,3,14,4,256]{4,3,2,1,0:T(4,128)(2,1)S(1)} %reshape.170, s32[]{:T(128)S(6)} %select_n.259, s32[]{:T(128)S(6)} %select_n.261), kind=kLoop, calls=%fused_computation | loop fusion | bytes 5308432 | tf_op jit(solution)/shard_map/dynamic_slice | solution.py:69
  125.7 3.8 %fusion = bf16[16,5,12,4,144]{4,3,2,1,0:T(4,128)(2,1)S(1)} fusion(s32[]{:T(128)S(6)} %select_n.266, bf16[16,5,12,4,256]{4,3,2,1,0:T(4,128)(2,1)S(1)} %get-tuple-element.12, bf16[16,5,12,4,256]{4,3,2,1,0:T(4,128)(2,1)S(1)} %get-tuple-element.11), kind=kLoop, calls=%fused_computation.4 | loop fusion | flops 2211840 | bytes 5038084 | tf_op jit(solution)/shard_map/concatenate | solution.py:75
  129.5 2.1 %fusion.30 = (bf16[16,3,12,4,144]{4,3,2,1,0:T(4,128)(2,1)}, bf16[16,3,12,4,144]{4,3,2,1,0:T(4,128)(2,1)S(1)}, bf16[16,3,12,4,144]{4,3,2,1,0:T(4,128)(2,1)S(1)}) fusion(bf16[16,5,12,4,144]{4,3,2,1,0:T(4,128)(2,1)S(1)} %fusion), kind=kLoop, calls=%fused_computation.210 | loop fusion | bytes 3981312 | tf_op jit(solution)/shard_map/slice | solution.py:81
  131.6 3.2 %reshape.171 = bf16[2304,144]{1,0:T(8,128)(2,1)} reshape(bf16[16,3,12,4,144]{4,3,2,1,0:T(4,128)(2,1)} %get-tuple-element.8) | data formatting | bytes 1327104 | tf_op jit(solution)/shard_map/reshape | solution.py:81
  134.7 1.7 %convolution_bitcast_fusion.2 = f32[1,1,144,256]{3,2,1,0:T(8,128)S(1)} fusion(bf16[2304,144]{1,0:T(8,128)(2,1)} %reshape.171, bf16[2304,256]{1,0:T(8,128)(2,1)S(1)} %bitcast.86), kind=kOutput, calls=%fused_computation.11 | convolution fusion | flops 169869312 | bytes 1990656 | tf_op jit(solution)/shard_map/dot_general | solution.py:80
  136.5 0.8 copy.46
  137.3 1.6 %reshape.173 = bf16[2304,144]{1,0:T(8,128)(2,1)} reshape(bf16[16,3,12,4,144]{4,3,2,1,0:T(4,128)(2,1)S(1)} %get-tuple-element.9) | data formatting | bytes 1327104 | tf_op jit(solution)/shard_map/reshape | solution.py:81
  138.8 1.7 %convolution_bitcast_fusion.1 = f32[1,1,144,256]{3,2,1,0:T(8,128)S(1)} fusion(bf16[2304,144]{1,0:T(8,128)(2,1)} %reshape.173, bf16[2304,256]{1,0:T(8,128)(2,1)S(1)} %bitcast.87), kind=kOutput, calls=%fused_computation.10 | convolution fusion | flops 169869312 | bytes 1990656 | tf_op jit(solution)/shard_map/dot_general | solution.py:80
  140.6 0.8 copy.47
  141.4 0.7 reshape.174
  142.2 0.5 convolution_bitcast_fusion
  142.6 0.2 copy.48
  142.8 0.3 copy-done.3
  143.1 0.4 pad_maximum_fusion
  143.5 1.1 broadcast_in_dim.60
  (129 shorter events, 3.0 us)
Async XLA Ops:
  7.2 108.2 %all-gather.3.cloned.1.call-start = ((), (), s32[]{:S(2)}) async-start(), calls=%async_computation | async-start | bytes 2715648 | tf_op jit(solution)/shard_map/all_gather | solution.py:57
  9.6 0.6 copy-start.5
  10.3 15.7 %collective-permute-start.5 = (bf16[1,3,2,4,256]{4,2,3,1,0:T(2,128)(2,1)S(1)}, bf16[1,3,2,4,256]{4,2,3,1,0:T(2,128)(2,1)}, u32[]{:S(2)}, u32[]{:S(2)}) collective-permute-start(bf16[1,3,2,4,256]{4,2,3,1,0:T(2,128)(2,1)S(1)} %maximum_bitcast_fusion.2), channel_id=1, source_target_pairs={{0,1},{1,0},{2,3},{3,2},{4,5},{5,4},{6,7},{7,6},{8,9},{9,8},{10,11... | collective-permute-start | bytes 36872 | tf_op jit(solution)/shard_map/ppermute | solution.py:11
  14.3 0.6 copy-start.6
  15.6 13.3 %collective-permute-start = (bf16[1,3,2,4,256]{4,2,3,1,0:T(2,128)(2,1)}, bf16[1,3,2,4,256]{4,2,3,1,0:T(2,128)(2,1)}, u32[]{:S(2)}, u32[]{:S(2)}) collective-permute-start(bf16[1,3,2,4,256]{4,2,3,1,0:T(2,128)(2,1)} %maximum_bitcast_fusion), channel_id=1, source_target_pairs={{0,1},{1,0},{2,3},{3,2},{4,5},{5,4},{6,7},{7,6},{8,9},{9,8},{10,11... | collective-permute-start | bytes 36872 | tf_op jit(solution)/shard_map/ppermute | solution.py:11
  26.8 3.9 %collective-permute-start.6 = (bf16[2,3,2,4,256]{4,2,3,1,0:T(2,128)(2,1)S(1)}, bf16[2,3,2,4,256]{4,2,3,1,0:T(2,128)(2,1)S(1)}, u32[]{:S(2)}, u32[]{:S(2)}) collective-permute-start(bf16[2,3,2,4,256]{4,2,3,1,0:T(2,128)(2,1)S(1)} %broadcast_select_fusion.4), channel_id=1, source_target_pairs={{0,2},{1,3},{2,0},{3,1},{4,6},{5,7},{6,4},{7,5},{8,10},{9,11},{10,... | collective-permute-start | bytes 73736 | tf_op jit(solution)/shard_map/ppermute | solution.py:11
  29.8 3.9 %collective-permute-start.1 = (bf16[2,3,2,4,256]{4,2,3,1,0:T(2,128)(2,1)S(1)}, bf16[2,3,2,4,256]{4,2,3,1,0:T(2,128)(2,1)S(1)}, u32[]{:S(2)}, u32[]{:S(2)}) collective-permute-start(bf16[2,3,2,4,256]{4,2,3,1,0:T(2,128)(2,1)S(1)} %broadcast_select_fusion.6), channel_id=1, source_target_pairs={{0,2},{1,3},{2,0},{3,1},{4,6},{5,7},{6,4},{7,5},{8,10},{9,11},{10,... | collective-permute-start | bytes 73736 | tf_op jit(solution)/shard_map/ppermute | solution.py:11
  35.8 2.0 %copy-start = (bf16[1,27,256,256]{3,2,1,0:T(8,128)(2,1)S(1)}, bf16[1,27,256,256]{3,2,1,0:T(8,128)(2,1)}, u32[]{:S(2)}) copy-start(bf16[1,27,256,256]{3,2,1,0:T(8,128)(2,1)} %param.8) | copy-start | bytes 10616836
  35.9 2.0 %copy-start.8 = (bf16[1,1,3,12,4,256]{5,4,3,2,1,0:T(4,128)(2,1)S(1)}, bf16[1,1,3,12,4,256]{5,4,3,2,1,0:T(4,128)(2,1)}, u32[]{:S(2)}) copy-start(bf16[1,1,3,12,4,256]{5,4,3,2,1,0:T(4,128)(2,1)} %param.6) | copy-start | bytes 221188
  37.9 3.3 %copy-start.2 = (bf16[27,256,256]{1,2,0:T(8,128)(2,1)S(1)}, bf16[27,256,256]{1,2,0:T(8,128)(2,1)}, u32[]{:S(2)}) copy-start(bf16[27,256,256]{1,2,0:T(8,128)(2,1)} %rev.3) | copy-start | bytes 10616836
  37.9 3.3 %copy-start.7 = (bf16[1,1,3,12,4,256]{5,4,3,2,1,0:T(4,128)(2,1)S(1)}, bf16[1,1,3,12,4,256]{5,4,3,2,1,0:T(4,128)(2,1)}, u32[]{:S(2)}) copy-start(bf16[1,1,3,12,4,256]{5,4,3,2,1,0:T(4,128)(2,1)} %param.7) | copy-start | bytes 221188
  38.7 2.4 %collective-permute-start.2 = (bf16[3,12,4,256]{3,1,2,0:T(8,128)(2,1)S(1)}, bf16[3,12,4,256]{3,1,2,0:T(8,128)(2,1)S(1)}, u32[]{:S(2)}, u32[]{:S(2)}) collective-permute-start(bf16[3,12,4,256]{3,1,2,0:T(8,128)(2,1)S(1)} %fusion.3), channel_id=1, source_target_pairs={{0,16},{1,17},{2,18},{3,19},{4,20},{5,21},{6,22},{7,23},{8,24},{9,... | collective-permute-start | bytes 221192 | tf_op jit(solution)/shard_map/ppermute | solution.py:22
  42.2 3.8 %collective-permute-start.3 = (bf16[1,3,2,4,256]{4,2,3,1,0:T(2,128)(2,1)S(1)}, bf16[1,3,2,4,256]{4,2,3,1,0:T(2,128)(2,1)S(1)}, u32[]{:S(2)}, u32[]{:S(2)}) collective-permute-start(bf16[1,3,2,4,256]{4,2,3,1,0:T(2,128)(2,1)S(1)} %maximum_bitcast_fusion.1), channel_id=1, source_target_pairs={{0,1},{1,0},{2,3},{3,2},{4,5},{5,4},{6,7},{7,6},{8,9},{9,8},{10,11... | collective-permute-start | bytes 36872 | tf_op jit(solution)/shard_map/ppermute | solution.py:11
  46.0 3.9 %collective-permute-start.4 = (bf16[2,3,2,4,256]{4,2,3,1,0:T(2,128)(2,1)S(1)}, bf16[2,3,2,4,256]{4,2,3,1,0:T(2,128)(2,1)S(1)}, u32[]{:S(2)}, u32[]{:S(2)}) collective-permute-start(bf16[2,3,2,4,256]{4,2,3,1,0:T(2,128)(2,1)S(1)} %broadcast_select_fusion.5), channel_id=1, source_target_pairs={{0,2},{1,3},{2,0},{3,1},{4,6},{5,7},{6,4},{7,5},{8,10},{9,11},{10,... | collective-permute-start | bytes 73736 | tf_op jit(solution)/shard_map/ppermute | solution.py:11
  46.1 4.3 %collective-permute-start.7 = (bf16[3,12,4,256]{3,1,2,0:T(8,128)(2,1)S(1)}, bf16[3,12,4,256]{3,1,2,0:T(8,128)(2,1)S(1)}, u32[]{:S(2)}, u32[]{:S(2)}) collective-permute-start(bf16[3,12,4,256]{3,1,2,0:T(8,128)(2,1)S(1)} %get-tuple-element.13), channel_id=1, source_target_pairs={{16,0},{17,1},{18,2},{19,3},{20,4},{21,5},{22,6},{23,7},{24,8},{25... | collective-permute-start | bytes 221192 | tf_op jit(solution)/shard_map/ppermute | solution.py:22
  51.4 2.0 %copy-start.1 = (bf16[1,27,256,256]{3,2,1,0:T(8,128)(2,1)S(1)}, bf16[1,27,256,256]{3,2,1,0:T(8,128)(2,1)}, u32[]{:S(2)}) copy-start(bf16[1,27,256,256]{3,2,1,0:T(8,128)(2,1)} %param.8) | copy-start | bytes 10616836
  142.1 0.9 copy-start.3
  142.1 1.0 copy-start.4
Sparse Core Ops, SparseCore 0:
  51.3 64.0 all-gather.2
